TPU v7x, 512 devices: a whole 4x8x8 slice. The times are simulated.
512 devices in a mesh: rep: 4 (over z_lo), fsdp: 16 (over y, core), tp: 8 (over z_hi, x).
Axes of the slice: x: 4, y: 8, z: 8 (z_hi: 2, z_lo: 4; z = z_hi * 4 + z_lo), core: 2. Of those that a mesh axis runs over, the one named last changes fastest.
Arguments:
- delta_attn: float32 [4, 4, 768, 768], P('rep', None, 'fsdp', 'tp'), may hold values from -4 to 4
- delta_in: float32 [4, 768, 3072], P('rep', 'fsdp', 'tp'), may hold values from -4 to 4
- delta_out: float32 [4, 3072, 768], P('rep', 'fsdp', 'tp'), may hold values from -4 to 4
- delta_small: float32 [4, 1920], P('rep'), may hold values from -4 to 4
- emb_left: float32 [4, 8, 4016, 64], P('rep', 'tp', 'fsdp'), may hold values from -6 to 6
- emb_right: float32 [4, 64, 768], P('rep'), may hold values from -0.75 to 0.75
- anchor_attn: float32 [8, 294912], P('tp', 'fsdp'), may hold values from -6 to 6
- anchor_in: float32 [8, 294912], P('tp', 'fsdp'), may hold values from -6 to 6
- anchor_out: float32 [8, 294912], P('tp', 'fsdp'), may hold values from -6 to 6
- anchor_small: float32 [1920], P('fsdp'), may hold values from -6 to 6
- anchor_emb: float32 [8, 16, 4, 48192], P('tp', 'fsdp', 'rep'), may hold values from -6 to 6
- moment_attn: float32 [8, 294912], P('tp', 'fsdp'), may hold values from -4 to 4
- moment_in: float32 [8, 294912], P('tp', 'fsdp'), may hold values from -4 to 4
- moment_out: float32 [8, 294912], P('tp', 'fsdp'), may hold values from -4 to 4
- moment_small: float32 [1920], P('fsdp'), may hold values from -4 to 4
- moment_emb: float32 [8, 16, 4, 48192], P('tp', 'fsdp', 'rep'), may hold values from -4 to 4
Outputs:
- new_attn: float32 [4, 768, 768], P(None, 'fsdp', 'tp')
- new_in: float32 [768, 3072], P('fsdp', 'tp')
- new_out: float32 [3072, 768], P('fsdp', 'tp')
- new_small: float32 [1920], replicated
- new_emb: float32 [32128, 768], P('tp', 'fsdp')
- next_attn: float32 [8, 294912], P('tp', 'fsdp')
- next_in: float32 [8, 294912], P('tp', 'fsdp')
- next_out: float32 [8, 294912], P('tp', 'fsdp')
- next_small: float32 [1920], P('fsdp')
- next_emb: float32 [8, 16, 4, 48192], P('tp', 'fsdp', 'rep')
All inputs are finite; a program needn't handle non-finite values.
Results may differ from a plain program's by a relative error of at most 0.000071.
Values sent between devices are 32-bit elements; how exact they have to be, the bound alone decides.
A program may use at most 64 MiB of HBM per device.

v0:
```python
import jax
import jax.numpy as jnp
from jax import lax
from jax.sharding import PartitionSpec as P

OUTER_RATE = 0.7
MOMENTUM_COEF = 0.9


def nesterov(anchor, moment, mean_delta):
    moment_next = MOMENTUM_COEF * moment + mean_delta
    updated = anchor - OUTER_RATE * (mean_delta + MOMENTUM_COEF * moment_next)
    return (updated, moment_next)


def to_blocks(matrix, lead, shards):
    local_rows = matrix.shape[-2]
    width = matrix.shape[-1] // shards
    shaped = matrix.reshape(lead, local_rows, shards, width)
    return jnp.transpose(shaped, (2, 3, 0, 1))


def from_blocks(blocks):
    shards, width, lead, local_rows = blocks.shape
    return jnp.transpose(blocks, (2, 3, 0, 1)).reshape(lead, local_rows, shards * width)


def on_device(
    delta_attn,
    delta_in,
    delta_out,
    delta_small,
    emb_left,
    emb_right,
    anchor_attn,
    anchor_in,
    anchor_out,
    anchor_small,
    anchor_emb,
    moment_attn,
    moment_in,
    moment_out,
    moment_small,
    moment_emb,
):
    groups = lax.axis_size("rep")
    shards = lax.axis_size("fsdp")
    send_attn = to_blocks(delta_attn[0], 4, shards)
    send_in = to_blocks(delta_in[0][None], 1, shards)
    send_out = to_blocks(delta_out[0][None], 1, shards)
    flat_attn, flat_in, flat_out = (
        lax.all_to_all(send_attn, "fsdp", split_axis=0, concat_axis=3, tiled=True),
        lax.all_to_all(send_in, "fsdp", split_axis=0, concat_axis=3, tiled=True),
        lax.all_to_all(send_out, "fsdp", split_axis=0, concat_axis=3, tiled=True),
    )
    block_shapes = (flat_attn.shape, flat_in.shape, flat_out.shape)
    portion = anchor_small.shape[0]
    small_local = lax.dynamic_slice_in_dim(
        delta_small[0], lax.axis_index("fsdp") * portion, portion, 0
    )[None, :]
    differences = (
        flat_attn.reshape(flat_attn.shape[1] * flat_attn.shape[2], flat_attn.shape[3]),
        flat_in.reshape(flat_in.shape[1], flat_in.shape[3]),
        flat_out.reshape(flat_out.shape[1], flat_out.shape[3]),
        small_local,
    )
    anchors = (
        anchor_attn.reshape(differences[0].shape),
        anchor_in.reshape(differences[1].shape),
        anchor_out.reshape(differences[2].shape),
        anchor_small[None, :],
    )
    moments = (
        moment_attn.reshape(differences[0].shape),
        moment_in.reshape(differences[1].shape),
        moment_out.reshape(differences[2].shape),
        moment_small[None, :],
    )
    totals = lax.psum((differences[0], differences[1], differences[2], differences[3]), "rep")
    updated_list = []
    moment_list = []
    for summed, anchor_part, moment_part in zip(totals, anchors, moments):
        updated, moment_next = nesterov(anchor_part, moment_part, summed / groups)
        updated_list.append(updated)
        moment_list.append(moment_next)
    back_attn = updated_list[0].reshape(block_shapes[0])
    back_in = updated_list[1].reshape(block_shapes[1])
    back_out = updated_list[2].reshape(block_shapes[2])
    train_attn, train_in, train_out = (
        lax.all_to_all(back_attn, "fsdp", split_axis=3, concat_axis=0, tiled=True),
        lax.all_to_all(back_in, "fsdp", split_axis=3, concat_axis=0, tiled=True),
        lax.all_to_all(back_out, "fsdp", split_axis=3, concat_axis=0, tiled=True),
    )
    new_attn = from_blocks(train_attn)
    new_in = from_blocks(train_in)[0]
    new_out = from_blocks(train_out)[0]
    new_small = lax.all_gather(updated_list[3].reshape(portion), "fsdp", axis=0, tiled=True)
    left_local = emb_left[0, 0]
    right_local = emb_right[0]
    block_rows = left_local.shape[0]
    column_count = right_local.shape[1] // groups
    product_term = jnp.dot(
        left_local, right_local, precision=lax.Precision.HIGHEST, preferred_element_type=jnp.float32
    )
    summed_emb = lax.psum_scatter(product_term, "rep", scatter_dimension=1, tiled=True)
    anchor_rows = anchor_emb[0, 0, 0].reshape(block_rows, column_count)
    moment_rows = moment_emb[0, 0, 0].reshape(block_rows, column_count)
    new_emb_part, next_emb_part = nesterov(anchor_rows, moment_rows, summed_emb / groups)
    full_rows = lax.all_gather(new_emb_part, "rep", axis=1, tiled=True)
    new_emb = lax.all_to_all(full_rows, "fsdp", split_axis=1, concat_axis=0, tiled=True)
    return (
        new_attn,
        new_in,
        new_out,
        new_small,
        new_emb,
        moment_list[0].reshape(moment_attn.shape),
        moment_list[1].reshape(moment_in.shape),
        moment_list[2].reshape(moment_out.shape),
        moment_list[3].reshape(moment_small.shape),
        next_emb_part.reshape(moment_emb.shape),
    )


def solution(mesh):
    placed = (
        P("rep", None, "fsdp", "tp"),
        P("rep", "fsdp", "tp"),
        P("rep", "fsdp", "tp"),
        P("rep", None),
        P("rep", "tp", "fsdp", None),
        P("rep", None, None),
        P("tp", "fsdp"),
        P("tp", "fsdp"),
        P("tp", "fsdp"),
        P("fsdp"),
        P("tp", "fsdp", "rep", None),
        P("tp", "fsdp"),
        P("tp", "fsdp"),
        P("tp", "fsdp"),
        P("fsdp"),
        P("tp", "fsdp", "rep", None),
    )
    return jax.shard_map(
        on_device,
        mesh=mesh,
        in_specs=placed,
        out_specs=(
            P(None, "fsdp", "tp"),
            P("fsdp", "tp"),
            P("fsdp", "tp"),
            P(),
            P("tp", "fsdp"),
            P("tp", "fsdp"),
            P("tp", "fsdp"),
            P("tp", "fsdp"),
            P("fsdp"),
            P("tp", "fsdp", "rep", None),
        ),
        check_vma=False,
    )
```

profile of v0, /device:TPU:32, one launch (start us, length us, event | category | flops | bytes accessed | tf_op | source)
XLA Modules:
  0.0 245.8 jit_solution(11660199578842059813)
XLA Ops:
  7.2 1.1 copy.88
  8.2 0.8 reshape.155
  9.1 8.8 %all-to-all-start.2 = ((f32[16,1,1152]{2,1,0:T(1,128)}), f32[16,1,1152]{2,1,0:T(1,128)S(1)}, u32[]{:S(2)}, u32[]{:S(2)}) async-start(f32[16,1,1152]{2,1,0:T(1,128)} %reshape.155), calls=%async_computation.2 | async-start | bytes 147456 | tf_op jit(solution)/shard_map/all_to_all | solution.py:53
  17.9 1.0 copy.83
  18.9 0.9 reshape.151
  19.8 1.4 all-to-all-done.2
  21.2 8.2 %all-to-all-start = ((f32[16,1,1152]{2,1,0:T(1,128)}), f32[16,1,1152]{2,1,0:T(1,128)S(1)}, u32[]{:S(2)}, u32[]{:S(2)}) async-start(f32[16,1,1152]{2,1,0:T(1,128)} %reshape.151), calls=%async_computation | async-start | bytes 147456 | tf_op jit(solution)/shard_map/all_to_all | solution.py:52
  29.3 1.6 copy.94
  31.5 0.8 reduce.28
  32.6 8.2 %all-to-all-start.4 = ((f32[16,6,1,192]{3,2,1,0:T(1,128)}), f32[16,6,1,192]{3,2,1,0:T(1,128)S(1)}, u32[]{:S(2)}, u32[]{:S(2)}) async-start(f32[16,6,1,192]{3,2,1,0:T(1,128)} %bitcast.21), calls=%async_computation.4 | async-start | bytes 196608 | tf_op jit(solution)/shard_map/all_to_all | solution.py:54
  40.9 0.8 reshape.93
  41.6 0.8 reduce.27
  42.7 0.8 reshape.89
  43.5 1.1 all-to-all-done.4
  45.6 1.7 fusion
  47.9 0.8 reduce.26
  49.2 0.8 reduce.25
  51.4 0.8 reduce.24
  55.1 0.8 copy.99
  55.9 48.3 %all-reduce.4.cloned.1.call-done = (f32[24,768]{1,0:T(8,128)}, f32[24,768]{1,0:T(8,128)}, f32[6,3072]{1,0:T(8,128)}) async-done(((f32[24,768]{1,0:T(8,128)}, f32[24,768]{1,0:T(8,128)}, f32[6,3072]{1,0:T(8,128)}), (f32[24,768]{1,0:T(8,128)}, f32[24,768]{1,0:T(8,128)}, f32[6,3072]{1,0:T(8,128)})) %all-reduce.4.cloned.1.call-update) | async-done | bytes 221200 | tf_op jit(solution)/shard_map/psum | solution.py:79
  104.1 1.6 fusion.2
  105.7 1.6 copy.96
  107.3 13.7 %reduce.32 = f32[3072,6]{1,0:T(8,128)S(1)} reduce(f32[3072,1,1,6]{3,2,1,0:T(1,128)S(1)} %bitcast.106, f32[]{:T(128)} %broadcast.90), dimensions={1,2}, to_apply=%bitcast.99.reduce_sub_computation | reduce | bytes 147460
  121.1 1.9 reshape.159
  123.0 7.2 %all-to-all-start.5 = ((f32[16,1,1152]{2,1,0:T(1,128)}), f32[16,1,1152]{2,1,0:T(1,128)S(1)}, u32[]{:S(2)}, u32[]{:S(2)}) async-start(f32[16,1,1152]{2,1,0:T(1,128)} %reshape.159), calls=%async_computation.5 | async-start | bytes 147456 | tf_op jit(solution)/shard_map/all_to_all | solution.py:92
  131.2 1.6 reduce.30
  132.8 0.9 reshape.157
  135.1 2.5 %reshape.153 = f32[16,1,1152]{2,1,0:T(1,128)} reshape(f32[768,1,4,6]{3,2,1,0:T(4,128)S(1)} %bitcast.103) | data formatting | bytes 147456
  137.6 7.2 %all-to-all-start.3 = ((f32[16,1,1152]{2,1,0:T(1,128)}), f32[16,1,1152]{2,1,0:T(1,128)S(1)}, u32[]{:S(2)}, u32[]{:S(2)}) async-start(f32[16,1,1152]{2,1,0:T(1,128)} %reshape.157), calls=%async_computation.3 | async-start | bytes 147456 | tf_op jit(solution)/shard_map/all_to_all | solution.py:91
  144.9 1.0 multiply_add_fusion
  145.9 2.2 all-to-all-done.3
  148.1 8.1 %all-to-all-start.1 = ((f32[16,1,1152]{2,1,0:T(1,128)}), f32[16,1,1152]{2,1,0:T(1,128)S(1)}, u32[]{:S(2)}, u32[]{:S(2)}) async-start(f32[16,1,1152]{2,1,0:T(1,128)} %reshape.153), calls=%async_computation.1 | async-start | bytes 147456 | tf_op jit(solution)/shard_map/all_to_all | solution.py:90
  156.3 18.3 %all_gather.7 = f32[251,768]{0,1:T(8,128)} all-gather(f32[251,192]{0,1:T(8,128)S(1)} %get-tuple-element.54), channel_id=1, replica_groups=mesh['rep'=4,'fsdp'=16,'tp'=8] {'rep'}, dimensions={1}, use_global_device_ids=true | all-gather | bytes 963840 | tf_op jit(solution)/shard_map/all_gather | solution.py:109
  174.6 7.2 %all-to-all-start.6 = ((f32[251,16,48]{0,2,1:T(8,128)}), f32[251,16,48]{0,2,1:T(8,128)S(1)}, u32[]{:S(2)}, u32[]{:S(2)}) async-start(f32[251,16,48]{0,2,1:T(8,128)} %bitcast.35), calls=%async_computation.7 | async-start | bytes 1572864 | tf_op jit(solution)/shard_map/all_to_all | solution.py:110
  181.8 1.3 dynamic-slice.1
  183.7 0.8 constant_dynamic-slice_fusion
  184.5 10.2 %psum.31 = f32[1,120]{1,0:T(1,128)S(1)} all-reduce(f32[1,120]{1,0:T(1,128)S(1)} %constant_dynamic-slice_fusion), channel_id=1, replica_groups=mesh['rep'=4,'fsdp'=16,'tp'=8] {'rep'}, use_global_device_ids=true, to_apply=%region_3.0 | all-reduce | flops 120 | bytes 960 | tf_op jit(solution)/shard_map/psum | solution.py:79
  194.8 26.9 %all-reduce = f32[1920]{0:T(1024)} all-reduce(f32[1920]{0:T(1024)S(1)} %bitcast_dynamic-update-slice_fusion), channel_id=2, replica_groups=mesh['rep'=4,'fsdp'=16,'tp'=8] {'fsdp'}, use_global_device_ids=true, to_apply=%add | all-reduce | flops 1920 | bytes 15360 | tf_op jit(solution)/shard_map/all_gather | solution.py:97
  224.4 0.8 reduce.33
  225.2 2.5 reshape.160
  229.1 0.8 reduce.31
  230.9 0.7 copy.104
  231.7 0.8 reduce.29
  232.5 2.0 reshape.154
  234.5 0.8 copy.106
  235.4 0.8 copy.103
  236.3 0.9 reshape.103
  237.7 1.3 all_to_all.110
  (100 shorter events, 15.6 us)
Async XLA Ops:
  7.2 38.4 %copy-start = (f32[1,64,768]{2,1,0:T(8,128)S(1)}, f32[1,64,768]{2,1,0:T(8,128)}, u32[]{:S(2)}) copy-start(f32[1,64,768]{2,1,0:T(8,128)} %param.21) | copy-start | bytes 589828
  9.1 12.1 %all-to-all-start.2 = ((f32[16,1,1152]{2,1,0:T(1,128)}), f32[16,1,1152]{2,1,0:T(1,128)S(1)}, u32[]{:S(2)}, u32[]{:S(2)}) async-start(f32[16,1,1152]{2,1,0:T(1,128)} %reshape.155), calls=%async_computation.2 | async-start | bytes 147456 | tf_op jit(solution)/shard_map/all_to_all | solution.py:53
  21.2 11.4 %all-to-all-start = ((f32[16,1,1152]{2,1,0:T(1,128)}), f32[16,1,1152]{2,1,0:T(1,128)S(1)}, u32[]{:S(2)}, u32[]{:S(2)}) async-start(f32[16,1,1152]{2,1,0:T(1,128)} %reshape.151), calls=%async_computation | async-start | bytes 147456 | tf_op jit(solution)/shard_map/all_to_all | solution.py:52
  32.3 13.3 %copy-start.21 = (f32[1,1,251,64]{2,3,1,0:T(8,128)S(1)}, f32[1,1,251,64]{2,3,1,0:T(8,128)}, u32[]{:S(2)}) copy-start(f32[1,1,251,64]{2,3,1,0:T(8,128)} %param.20) | copy-start | bytes 192772
  32.6 12.0 %all-to-all-start.4 = ((f32[16,6,1,192]{3,2,1,0:T(1,128)}), f32[16,6,1,192]{3,2,1,0:T(1,128)S(1)}, u32[]{:S(2)}, u32[]{:S(2)}) async-start(f32[16,6,1,192]{3,2,1,0:T(1,128)} %bitcast.21), calls=%async_computation.4 | async-start | bytes 196608 | tf_op jit(solution)/shard_map/all_to_all | solution.py:54
  40.8 63.4 %all-reduce.4.cloned.1.call-start = ((), (), s32[]{:S(2)}) async-start(), calls=%async_computation.9 | async-start | bytes 491520 | tf_op jit(solution)/shard_map/psum | solution.py:79
  42.7 5.2 %copy-start.13 = (f32[1,18432]{1,0:T(1,128)S(1)}, f32[1,18432]{1,0:T(1,128)}, u32[]{:S(2)}) copy-start(f32[1,18432]{1,0:T(1,128)} %param.24) | copy-start | bytes 221188
  42.7 6.0 %copy-start.17 = (f32[1,18432]{1,0:T(1,128)S(1)}, f32[1,18432]{1,0:T(1,128)}, u32[]{:S(2)}) copy-start(f32[1,18432]{1,0:T(1,128)} %param.29) | copy-start | bytes 221188
  42.7 6.0 %copy-start.18 = (f32[1,18432]{1,0:T(1,128)S(1)}, f32[1,18432]{1,0:T(1,128)}, u32[]{:S(2)}) copy-start(f32[1,18432]{1,0:T(1,128)} %param.28) | copy-start | bytes 221188
  44.6 4.7 %copy-start.14 = (f32[1,18432]{1,0:T(1,128)S(1)}, f32[1,18432]{1,0:T(1,128)}, u32[]{:S(2)}) copy-start(f32[1,18432]{1,0:T(1,128)} %param.23) | copy-start | bytes 221188
  45.3 6.0 %copy-start.15 = (f32[1,18432]{1,0:T(1,128)S(1)}, f32[1,18432]{1,0:T(1,128)}, u32[]{:S(2)}) copy-start(f32[1,18432]{1,0:T(1,128)} %param.22) | copy-start | bytes 221188
  45.4 7.5 %copy-start.16 = (f32[1,18432]{1,0:T(1,128)S(1)}, f32[1,18432]{1,0:T(1,128)}, u32[]{:S(2)}) copy-start(f32[1,18432]{1,0:T(1,128)} %param.27) | copy-start | bytes 221188
  45.4 8.3 %copy-start.11 = (f32[1,1,1,48192]{3,2,1,0:T(1,128)S(1)}, f32[1,1,1,48192]{3,2,1,0:T(1,128)}, u32[]{:S(2)}) copy-start(f32[1,1,1,48192]{3,2,1,0:T(1,128)} %param.26) | copy-start | bytes 578308
  45.4 99.5 %reduce-scatter.2.cloned.1.call-start = ((), (), s32[]{:S(2)}) async-start(), calls=%async_computation.8 | async-start | bytes 983040 | tf_op jit(solution)/shard_map/reduce_scatter | solution.py:105
  47.4 7.0 %copy-start.12 = (f32[1,1,1,48192]{3,2,1,0:T(1,128)S(1)}, f32[1,1,1,48192]{3,2,1,0:T(1,128)}, u32[]{:S(2)}) copy-start(f32[1,1,1,48192]{3,2,1,0:T(1,128)} %param.31) | copy-start | bytes 578308
  121.0 9.2 %copy-start.9 = (f32[24,768]{1,0:T(8,128)S(1)}, f32[24,768]{1,0:T(8,128)}, u32[]{:S(2)}) copy-start(f32[24,768]{1,0:T(8,128)} %reshape.92) | copy-start | bytes 221188
  121.0 9.2 %copy-start.10 = (f32[24,768]{1,0:T(8,128)S(1)}, f32[24,768]{1,0:T(8,128)}, u32[]{:S(2)}) copy-start(f32[24,768]{1,0:T(8,128)} %mul.77) | copy-start | bytes 221188
  121.0 9.2 %copy-start.20 = (f32[24,768]{1,0:T(8,128)S(1)}, f32[24,768]{1,0:T(8,128)}, u32[]{:S(2)}) copy-start(f32[24,768]{1,0:T(8,128)} %get-tuple-element.51) | copy-start | bytes 221188
  121.0 12.7 %copy-start.7 = (f32[24,768]{1,0:T(8,128)S(1)}, f32[24,768]{1,0:T(8,128)}, u32[]{:S(2)}) copy-start(f32[24,768]{1,0:T(8,128)} %reshape.88) | copy-start | bytes 221188
  121.0 12.7 %copy-start.8 = (f32[24,768]{1,0:T(8,128)S(1)}, f32[24,768]{1,0:T(8,128)}, u32[]{:S(2)}) copy-start(f32[24,768]{1,0:T(8,128)} %mul.73) | copy-start | bytes 221188
  121.0 12.7 %copy-start.19 = (f32[24,768]{1,0:T(8,128)S(1)}, f32[24,768]{1,0:T(8,128)}, u32[]{:S(2)}) copy-start(f32[24,768]{1,0:T(8,128)} %get-tuple-element.50) | copy-start | bytes 221188
  123.0 14.6 %all-to-all-start.5 = ((f32[16,1,1152]{2,1,0:T(1,128)}), f32[16,1,1152]{2,1,0:T(1,128)S(1)}, u32[]{:S(2)}, u32[]{:S(2)}) async-start(f32[16,1,1152]{2,1,0:T(1,128)} %reshape.159), calls=%async_computation.5 | async-start | bytes 147456 | tf_op jit(solution)/shard_map/all_to_all | solution.py:92
  134.4 10.5 %copy-start.1 = (f32[251,192]{0,1:T(8,128)S(1)}, f32[251,192]{0,1:T(8,128)}, u32[]{:S(2)}) copy-start(f32[251,192]{0,1:T(8,128)} %copy.99) | copy-start | bytes 578308
  137.6 10.5 %all-to-all-start.3 = ((f32[16,1,1152]{2,1,0:T(1,128)}), f32[16,1,1152]{2,1,0:T(1,128)S(1)}, u32[]{:S(2)}, u32[]{:S(2)}) async-start(f32[16,1,1152]{2,1,0:T(1,128)} %reshape.157), calls=%async_computation.3 | async-start | bytes 147456 | tf_op jit(solution)/shard_map/all_to_all | solution.py:91
  145.8 48.8 %copy-start.22 = (f32[120]{0:T(128)S(1)}, f32[120]{0:T(128)}, u32[]{:S(2)}) copy-start(f32[120]{0:T(128)} %param.25) | copy-start | bytes 1444
  145.9 48.8 %copy-start.23 = (f32[120]{0:T(128)S(1)}, f32[120]{0:T(128)}, u32[]{:S(2)}) copy-start(f32[120]{0:T(128)} %param.30) | copy-start | bytes 1444
  145.9 76.3 %copy-start.2 = (f32[1,1,6,3072]{3,2,1,0:T(8,128)S(1)}, f32[1,1,6,3072]{3,2,1,0:T(8,128)}, u32[]{:S(2)}) copy-start(f32[1,1,6,3072]{3,2,1,0:T(8,128)} %get-tuple-element.55) | copy-start | bytes 221188
  145.9 77.0 %copy-start.5 = (f32[1,1,24,768]{3,2,1,0:T(8,128)S(1)}, f32[1,1,24,768]{3,2,1,0:T(8,128)}, u32[]{:S(2)}) copy-start(f32[1,1,24,768]{3,2,1,0:T(8,128)} %get-tuple-element.57) | copy-start | bytes 221188
  145.9 77.7 %copy-start.6 = (f32[1,1,24,768]{3,2,1,0:T(8,128)S(1)}, f32[1,1,24,768]{3,2,1,0:T(8,128)}, u32[]{:S(2)}) copy-start(f32[1,1,24,768]{3,2,1,0:T(8,128)} %get-tuple-element.59) | copy-start | bytes 221188
  148.1 76.2 %copy-start.3 = (f32[16,1,1152]{2,1,0:T(1,128)}, f32[16,1,1152]{2,1,0:T(1,128)S(1)}, u32[]{:S(2)}) copy-start(f32[16,1,1152]{2,1,0:T(1,128)S(1)} %all-to-all-done.3) | copy-start | bytes 221188
  148.1 26.4 %all-to-all-start.1 = ((f32[16,1,1152]{2,1,0:T(1,128)}), f32[16,1,1152]{2,1,0:T(1,128)S(1)}, u32[]{:S(2)}, u32[]{:S(2)}) async-start(f32[16,1,1152]{2,1,0:T(1,128)} %reshape.153), calls=%async_computation.1 | async-start | bytes 147456 | tf_op jit(solution)/shard_map/all_to_all | solution.py:90
  174.6 62.6 %all-to-all-start.6 = ((f32[251,16,48]{0,2,1:T(8,128)}), f32[251,16,48]{0,2,1:T(8,128)S(1)}, u32[]{:S(2)}, u32[]{:S(2)}) async-start(f32[251,16,48]{0,2,1:T(8,128)} %bitcast.35), calls=%async_computation.7 | async-start | bytes 1572864 | tf_op jit(solution)/shard_map/all_to_all | solution.py:110
  227.6 1.5 copy-start.4
Sparse Core Ops, SparseCore 0:
  45.5 58.6 all-reduce.3
  107.8 30.1 reduce-scatter.1
where the time goes:
time: 247 us; the launch traced here: 246 us
  blocking collectives  55.4 us (22%)
  starting transfers between devices  55.2 us (22%)
  waiting for transfers between devices  53.1 us (21%)
  local copies, waits for them, and re-layouts  37.2 us (15%)
  other arithmetic  27.9 us (11%)
  between operations  15.3 us (6%)
    psum x1, waiting for transfers between devices, on_device(): lax.psum((differences[0], differences[1], differences[2], differences[3])...  48.3 us
    all_gather x1, blocking collectives, on_device(): lax.all_gather(updated_list[3].reshape(portion), 'fsdp', axis=0, tiled=True)  26.9 us
    unnamed x70, local copies, waits for them, and re-layouts  22.5 us
    unnamed x10, other arithmetic  21.2 us
    all_gather x1, blocking collectives, on_device(): full_rows = lax.all_gather(new_emb_part, 'rep', axis=1, tiled=True)  18.3 us
    psum x1, blocking collectives, on_device(): lax.psum((differences[0], differences[1], differences[2], differences[3])...  10.2 us
    all_to_all x1, starting transfers between devices, on_device(): lax.all_to_all(send_in, 'fsdp', split_axis=0, concat_axis=3, tiled=True)  8.82 us
    all_to_all x1, starting transfers between devices, on_device(): lax.all_to_all(send_out, 'fsdp', split_axis=0, concat_axis=3, tiled=True)  8.17 us
  transfers between devices with their start and end apart: 9, of which 5 were waited for; matrix products, arithmetic and copies ran while one was open for 25% of the time, Pallas kernels for 0%

commit v1 on v0

--- a/solution.py
+++ b/solution.py
@@ -5,6 +5,19 @@
 
 OUTER_RATE = 0.7
 MOMENTUM_COEF = 0.9
+
+
+def collect(value, axis, dim):
+    ways = lax.axis_size(axis)
+    up = [(d, (d + 1) % ways) for d in range(ways)]
+    down = [(d, (d - 1) % ways) for d in range(ways)]
+    earlier, later = ([value], [value])
+    for _ in range(ways // 2):
+        earlier.append(lax.ppermute(earlier[-1], axis, up))
+    for _ in range((ways - 1) // 2):
+        later.append(lax.ppermute(later[-1], axis, down))
+    line = jnp.concatenate([*earlier[::-1], *later[1:]], axis=dim)
+    return jnp.roll(line, (lax.axis_index(axis) - ways // 2) * value.shape[dim], axis=dim)
 
 
 def nesterov(anchor, moment, mean_delta):
@@ -94,7 +107,7 @@
     new_attn = from_blocks(train_attn)
     new_in = from_blocks(train_in)[0]
     new_out = from_blocks(train_out)[0]
-    new_small = lax.all_gather(updated_list[3].reshape(portion), "fsdp", axis=0, tiled=True)
+    new_small = collect(updated_list[3].reshape(portion), "fsdp", 0)
     left_local = emb_left[0, 0]
     right_local = emb_right[0]
     block_rows = left_local.shape[0]

time: 247 us -> 255 us (1.032)
  the two profiles are of different devices: /device:TPU:32 before, /device:TPU:2 now
where the time goes in v1:
time: 255 us; the launch traced here: 254 us
  waiting for transfers between devices  86.5 us (34%)
  starting transfers between devices  58.8 us (23%)
  local copies, waits for them, and re-layouts  36.7 us (14%)
  blocking collectives  28.5 us (11%)
  other arithmetic  27.3 us (11%)
  between operations  14.7 us (6%)
    psum x1, waiting for transfers between devices, on_device(): lax.psum((differences[0], differences[1], differences[2], differences[3])...  45.7 us
    unnamed x68, local copies, waits for them, and re-layouts  21.2 us
    unnamed x9, other arithmetic  20.9 us
    ppermute x7, starting transfers between devices, collect(): later.append(lax.ppermute(later[-1], axis, down))  20.3 us
    all_gather x1, blocking collectives, on_device(): full_rows = lax.all_gather(new_emb_part, 'rep', axis=1, tiled=True)  18.3 us
    ppermute x8, waiting for transfers between devices, collect(): earlier.append(lax.ppermute(earlier[-1], axis, up))  16.2 us
    psum x1, blocking collectives, on_device(): lax.psum((differences[0], differences[1], differences[2], differences[3])...  10.2 us
    all_to_all x1, starting transfers between devices, on_device(): lax.all_to_all(send_in, 'fsdp', split_axis=0, concat_axis=3, tiled=True)  7.21 us
  transfers between devices with their start and end apart: 24, of which 20 were waited for; matrix products, arithmetic and copies ran while one was open for 24% of the time, Pallas kernels for 0%

profile of v1, /device:TPU:2, one launch (start us, length us, event | category | flops | bytes accessed | tf_op | source)
XLA Modules:
  0.0 254.3 jit_solution(18218843272024619283)
XLA Ops:
  7.2 1.1 copy.88
  8.2 0.8 reshape.148
  9.1 7.2 %all-to-all-start.2 = ((f32[16,1,1152]{2,1,0:T(1,128)}), f32[16,1,1152]{2,1,0:T(1,128)S(1)}, u32[]{:S(2)}, u32[]{:S(2)}) async-start(f32[16,1,1152]{2,1,0:T(1,128)} %reshape.148), calls=%async_computation.2 | async-start | bytes 147456 | tf_op jit(solution)/shard_map/all_to_all | solution.py:66
  16.3 1.0 copy.83
  17.3 0.9 reshape.144
  18.2 6.1 %all-to-all-done.2 = f32[16,1,1152]{2,1,0:T(1,128)S(1)} async-done(((f32[16,1,1152]{2,1,0:T(1,128)}), f32[16,1,1152]{2,1,0:T(1,128)S(1)}, u32[]{:S(2)}, u32[]{:S(2)}) %all-to-all-start.2) | async-done | bytes 73760 | tf_op jit(solution)/shard_map/all_to_all | solution.py:66
  24.3 3.5 %all-to-all-start = ((f32[16,1,1152]{2,1,0:T(1,128)}), f32[16,1,1152]{2,1,0:T(1,128)S(1)}, u32[]{:S(2)}, u32[]{:S(2)}) async-start(f32[16,1,1152]{2,1,0:T(1,128)} %reshape.144), calls=%async_computation | async-start | bytes 147456 | tf_op jit(solution)/shard_map/all_to_all | solution.py:65
  27.8 1.6 copy.94
  30.8 4.9 %all-to-all-done = f32[16,1,1152]{2,1,0:T(1,128)S(1)} async-done(((f32[16,1,1152]{2,1,0:T(1,128)}), f32[16,1,1152]{2,1,0:T(1,128)S(1)}, u32[]{:S(2)}, u32[]{:S(2)}) %all-to-all-start) | async-done | bytes 73760 | tf_op jit(solution)/shard_map/all_to_all | solution.py:65
  35.7 3.5 %all-to-all-start.4 = ((f32[16,6,1,192]{3,2,1,0:T(1,128)}), f32[16,6,1,192]{3,2,1,0:T(1,128)S(1)}, u32[]{:S(2)}, u32[]{:S(2)}) async-start(f32[16,6,1,192]{3,2,1,0:T(1,128)} %bitcast.21), calls=%async_computation.4 | async-start | bytes 196608 | tf_op jit(solution)/shard_map/all_to_all | solution.py:67
  41.9 5.6 %all-to-all-done.4 = f32[16,6,1,192]{3,2,1,0:T(1,128)S(1)} async-done(((f32[16,6,1,192]{3,2,1,0:T(1,128)}), f32[16,6,1,192]{3,2,1,0:T(1,128)S(1)}, u32[]{:S(2)}, u32[]{:S(2)}) %all-to-all-start.4) | async-done | bytes 73760 | tf_op jit(solution)/shard_map/all_to_all | solution.py:67
  48.5 1.7 fusion
  52.2 0.8 reduce.25
  58.8 45.7 %all-reduce.3.cloned.1.call-done = (f32[24,768]{1,0:T(8,128)}, f32[24,768]{1,0:T(8,128)}, f32[6,3072]{1,0:T(8,128)}) async-done(((f32[24,768]{1,0:T(8,128)}, f32[24,768]{1,0:T(8,128)}, f32[6,3072]{1,0:T(8,128)}), (f32[24,768]{1,0:T(8,128)}, f32[24,768]{1,0:T(8,128)}, f32[6,3072]{1,0:T(8,128)})) %all-reduce.3.cloned.1.call-update) | async-done | bytes 221200 | tf_op jit(solution)/shard_map/psum | solution.py:92
  104.5 1.6 fusion.2
  106.0 1.6 copy.96
  107.7 13.6 %reduce.32 = f32[3072,6]{1,0:T(8,128)S(1)} reduce(f32[3072,1,1,6]{3,2,1,0:T(1,128)S(1)} %bitcast.105, f32[]{:T(128)} %broadcast.89), dimensions={1,2}, to_apply=%bitcast.98.reduce_sub_computation | reduce | bytes 147460
  121.3 1.9 reshape.152
  123.2 6.9 %all-to-all-start.5 = ((f32[16,1,1152]{2,1,0:T(1,128)}), f32[16,1,1152]{2,1,0:T(1,128)S(1)}, u32[]{:S(2)}, u32[]{:S(2)}) async-start(f32[16,1,1152]{2,1,0:T(1,128)} %reshape.152), calls=%async_computation.5 | async-start | bytes 147456 | tf_op jit(solution)/shard_map/all_to_all | solution.py:105
  131.1 1.5 reduce.30
  132.6 0.9 reshape.150
  135.0 2.5 reshape.146
  138.1 6.6 %all-to-all-start.3 = ((f32[16,1,1152]{2,1,0:T(1,128)}), f32[16,1,1152]{2,1,0:T(1,128)S(1)}, u32[]{:S(2)}, u32[]{:S(2)}) async-start(f32[16,1,1152]{2,1,0:T(1,128)} %reshape.150), calls=%async_computation.3 | async-start | bytes 147456 | tf_op jit(solution)/shard_map/all_to_all | solution.py:104
  144.7 1.0 multiply_add_fusion
  145.7 6.9 %all-to-all-done.3 = f32[16,1,1152]{2,1,0:T(1,128)S(1)} async-done(((f32[16,1,1152]{2,1,0:T(1,128)}), f32[16,1,1152]{2,1,0:T(1,128)S(1)}, u32[]{:S(2)}, u32[]{:S(2)}) %all-to-all-start.3) | async-done | bytes 73760 | tf_op jit(solution)/shard_map/all_to_all | solution.py:104
  152.6 3.5 %all-to-all-start.1 = ((f32[16,1,1152]{2,1,0:T(1,128)}), f32[16,1,1152]{2,1,0:T(1,128)S(1)}, u32[]{:S(2)}, u32[]{:S(2)}) async-start(f32[16,1,1152]{2,1,0:T(1,128)} %reshape.146), calls=%async_computation.1 | async-start | bytes 147456 | tf_op jit(solution)/shard_map/all_to_all | solution.py:103
  156.2 18.3 %all_gather.3 = f32[251,768]{0,1:T(8,128)} all-gather(f32[251,192]{0,1:T(8,128)S(1)} %get-tuple-element.54), channel_id=1, replica_groups=mesh['rep'=4,'fsdp'=16,'tp'=8] {'rep'}, dimensions={1}, use_global_device_ids=true | all-gather | bytes 963840 | tf_op jit(solution)/shard_map/all_gather | solution.py:122
  174.5 7.1 %all-to-all-start.6 = ((f32[251,16,48]{0,2,1:T(8,128)}), f32[251,16,48]{0,2,1:T(8,128)S(1)}, u32[]{:S(2)}, u32[]{:S(2)}) async-start(f32[251,16,48]{0,2,1:T(8,128)} %bitcast.34), calls=%async_computation.7 | async-start | bytes 1572864 | tf_op jit(solution)/shard_map/all_to_all | solution.py:123
  182.4 10.2 %psum.31 = f32[1,120]{1,0:T(1,128)S(1)} all-reduce(f32[1,120]{1,0:T(1,128)S(1)} %constant_dynamic-slice_fusion), channel_id=1, replica_groups=mesh['rep'=4,'fsdp'=16,'tp'=8] {'rep'}, use_global_device_ids=true, to_apply=%region_3.0 | all-reduce | flops 120 | bytes 960 | tf_op jit(solution)/shard_map/psum | solution.py:92
  193.1 3.0 %collective-permute-start.8 = (f32[120]{0:T(128)S(1)}, f32[120]{0:T(128)S(1)}, u32[]{:S(2)}, u32[]{:S(2)}) collective-permute-start(f32[120]{0:T(128)S(1)} %get-tuple-element.62), channel_id=1, source_target_pairs={{0,120},{8,0},{16,8},{24,16},{32,24},{40,32},{48,40},{56,48},{64,5... | collective-permute-start | bytes 1448 | tf_op jit(solution)/shard_map/ppermute | solution.py:18
  196.1 4.8 %collective-permute-done = f32[120]{0:T(128)S(1)} collective-permute-done((f32[120]{0:T(128)S(1)}, f32[120]{0:T(128)S(1)}, u32[]{:S(2)}, u32[]{:S(2)}) %collective-permute-start) | collective-permute-done | bytes 512 | tf_op jit(solution)/shard_map/ppermute | solution.py:16
  200.9 3.0 %collective-permute-start.9 = (f32[120]{0:T(128)S(1)}, f32[120]{0:T(128)S(1)}, u32[]{:S(2)}, u32[]{:S(2)}) collective-permute-start(f32[120]{0:T(128)S(1)} %collective-permute-done.8), channel_id=1, source_target_pairs={{0,120},{8,0},{16,8},{24,16},{32,24},{40,32},{48,40},{56,48},{64,5... | collective-permute-start | bytes 1448 | tf_op jit(solution)/shard_map/ppermute | solution.py:18
  203.8 1.2 collective-permute-done.1
  205.1 2.9 %collective-permute-start.10 = (f32[120]{0:T(128)S(1)}, f32[120]{0:T(128)S(1)}, u32[]{:S(2)}, u32[]{:S(2)}) collective-permute-start(f32[120]{0:T(128)S(1)} %collective-permute-done.9), channel_id=1, source_target_pairs={{0,120},{8,0},{16,8},{24,16},{32,24},{40,32},{48,40},{56,48},{64,5... | collective-permute-start | bytes 1448 | tf_op jit(solution)/shard_map/ppermute | solution.py:18
  208.0 1.2 collective-permute-done.2
  209.3 2.9 %collective-permute-start.11 = (f32[120]{0:T(128)S(1)}, f32[120]{0:T(128)S(1)}, u32[]{:S(2)}, u32[]{:S(2)}) collective-permute-start(f32[120]{0:T(128)S(1)} %collective-permute-done.10), channel_id=1, source_target_pairs={{0,120},{8,0},{16,8},{24,16},{32,24},{40,32},{48,40},{56,48},{64,5... | collective-permute-start | bytes 1448 | tf_op jit(solution)/shard_map/ppermute | solution.py:18
  212.2 1.2 collective-permute-done.3
  213.5 2.9 %collective-permute-start.12 = (f32[120]{0:T(128)S(1)}, f32[120]{0:T(128)S(1)}, u32[]{:S(2)}, u32[]{:S(2)}) collective-permute-start(f32[120]{0:T(128)S(1)} %collective-permute-done.11), channel_id=1, source_target_pairs={{0,120},{8,0},{16,8},{24,16},{32,24},{40,32},{48,40},{56,48},{64,5... | collective-permute-start | bytes 1448 | tf_op jit(solution)/shard_map/ppermute | solution.py:18
  216.3 1.2 collective-permute-done.4
  217.6 2.9 %collective-permute-start.13 = (f32[120]{0:T(128)S(1)}, f32[120]{0:T(128)S(1)}, u32[]{:S(2)}, u32[]{:S(2)}) collective-permute-start(f32[120]{0:T(128)S(1)} %collective-permute-done.12), channel_id=1, source_target_pairs={{0,120},{8,0},{16,8},{24,16},{32,24},{40,32},{48,40},{56,48},{64,5... | collective-permute-start | bytes 1448 | tf_op jit(solution)/shard_map/ppermute | solution.py:18
  220.5 1.2 collective-permute-done.5
  221.8 2.9 %collective-permute-start.14 = (f32[120]{0:T(128)S(1)}, f32[120]{0:T(128)S(1)}, u32[]{:S(2)}, u32[]{:S(2)}) collective-permute-start(f32[120]{0:T(128)S(1)} %collective-permute-done.13), channel_id=1, source_target_pairs={{0,120},{8,0},{16,8},{24,16},{32,24},{40,32},{48,40},{56,48},{64,5... | collective-permute-start | bytes 1448 | tf_op jit(solution)/shard_map/ppermute | solution.py:18
  224.7 1.2 collective-permute-done.6
  226.0 4.1 %collective-permute-done.7 = f32[120]{0:T(128)S(1)} collective-permute-done((f32[120]{0:T(128)S(1)}, f32[120]{0:T(128)S(1)}, u32[]{:S(2)}, u32[]{:S(2)}) %collective-permute-start.7) | collective-permute-done | bytes 512 | tf_op jit(solution)/shard_map/ppermute | solution.py:16
  233.8 2.5 reshape.153
  240.9 2.0 reshape.147
  244.7 0.9 reshape.103
  246.1 1.3 all_to_all.110
  (128 shorter events, 27.9 us)
Async XLA Ops:
  7.2 41.3 %copy-start = (f32[1,64,768]{2,1,0:T(8,128)S(1)}, f32[1,64,768]{2,1,0:T(8,128)}, u32[]{:S(2)}) copy-start(f32[1,64,768]{2,1,0:T(8,128)} %param.21) | copy-start | bytes 589828
  9.1 15.2 %all-to-all-start.2 = ((f32[16,1,1152]{2,1,0:T(1,128)}), f32[16,1,1152]{2,1,0:T(1,128)S(1)}, u32[]{:S(2)}, u32[]{:S(2)}) async-start(f32[16,1,1152]{2,1,0:T(1,128)} %reshape.148), calls=%async_computation.2 | async-start | bytes 147456 | tf_op jit(solution)/shard_map/all_to_all | solution.py:66
  24.3 11.4 %all-to-all-start = ((f32[16,1,1152]{2,1,0:T(1,128)}), f32[16,1,1152]{2,1,0:T(1,128)S(1)}, u32[]{:S(2)}, u32[]{:S(2)}) async-start(f32[16,1,1152]{2,1,0:T(1,128)} %reshape.144), calls=%async_computation | async-start | bytes 147456 | tf_op jit(solution)/shard_map/all_to_all | solution.py:65
  30.7 17.9 %copy-start.21 = (f32[1,1,251,64]{2,3,1,0:T(8,128)S(1)}, f32[1,1,251,64]{2,3,1,0:T(8,128)}, u32[]{:S(2)}) copy-start(f32[1,1,251,64]{2,3,1,0:T(8,128)} %param.20) | copy-start | bytes 192772
  35.7 11.8 %all-to-all-start.4 = ((f32[16,6,1,192]{3,2,1,0:T(1,128)}), f32[16,6,1,192]{3,2,1,0:T(1,128)S(1)}, u32[]{:S(2)}, u32[]{:S(2)}) async-start(f32[16,6,1,192]{3,2,1,0:T(1,128)} %bitcast.21), calls=%async_computation.4 | async-start | bytes 196608 | tf_op jit(solution)/shard_map/all_to_all | solution.py:67
  39.2 65.3 %all-reduce.3.cloned.1.call-start = ((), (), s32[]{:S(2)}) async-start(), calls=%async_computation.9 | async-start | bytes 491520 | tf_op jit(solution)/shard_map/psum | solution.py:92
  41.0 9.8 %copy-start.13 = (f32[1,18432]{1,0:T(1,128)S(1)}, f32[1,18432]{1,0:T(1,128)}, u32[]{:S(2)}) copy-start(f32[1,18432]{1,0:T(1,128)} %param.24) | copy-start | bytes 221188
  41.1 10.5 %copy-start.17 = (f32[1,18432]{1,0:T(1,128)S(1)}, f32[1,18432]{1,0:T(1,128)}, u32[]{:S(2)}) copy-start(f32[1,18432]{1,0:T(1,128)} %param.29) | copy-start | bytes 221188
  41.1 10.5 %copy-start.18 = (f32[1,18432]{1,0:T(1,128)S(1)}, f32[1,18432]{1,0:T(1,128)}, u32[]{:S(2)}) copy-start(f32[1,18432]{1,0:T(1,128)} %param.28) | copy-start | bytes 221188
  47.5 4.7 %copy-start.14 = (f32[1,18432]{1,0:T(1,128)S(1)}, f32[1,18432]{1,0:T(1,128)}, u32[]{:S(2)}) copy-start(f32[1,18432]{1,0:T(1,128)} %param.23) | copy-start | bytes 221188
  48.3 6.0 %copy-start.15 = (f32[1,18432]{1,0:T(1,128)S(1)}, f32[1,18432]{1,0:T(1,128)}, u32[]{:S(2)}) copy-start(f32[1,18432]{1,0:T(1,128)} %param.22) | copy-start | bytes 221188
  48.3 7.5 %copy-start.16 = (f32[1,18432]{1,0:T(1,128)S(1)}, f32[1,18432]{1,0:T(1,128)}, u32[]{:S(2)}) copy-start(f32[1,18432]{1,0:T(1,128)} %param.27) | copy-start | bytes 221188
  48.3 8.4 %copy-start.11 = (f32[1,1,1,48192]{3,2,1,0:T(1,128)S(1)}, f32[1,1,1,48192]{3,2,1,0:T(1,128)}, u32[]{:S(2)}) copy-start(f32[1,1,1,48192]{3,2,1,0:T(1,128)} %param.26) | copy-start | bytes 578308
  48.3 96.4 %reduce-scatter.2.cloned.1.call-start = ((), (), s32[]{:S(2)}) async-start(), calls=%async_computation.8 | async-start | bytes 983040 | tf_op jit(solution)/shard_map/reduce_scatter | solution.py:118
  50.3 7.0 %copy-start.12 = (f32[1,1,1,48192]{3,2,1,0:T(1,128)S(1)}, f32[1,1,1,48192]{3,2,1,0:T(1,128)}, u32[]{:S(2)}) copy-start(f32[1,1,1,48192]{3,2,1,0:T(1,128)} %param.31) | copy-start | bytes 578308
  121.3 8.8 %copy-start.9 = (f32[24,768]{1,0:T(8,128)S(1)}, f32[24,768]{1,0:T(8,128)}, u32[]{:S(2)}) copy-start(f32[24,768]{1,0:T(8,128)} %reshape.92) | copy-start | bytes 221188
  121.3 8.8 %copy-start.10 = (f32[24,768]{1,0:T(8,128)S(1)}, f32[24,768]{1,0:T(8,128)}, u32[]{:S(2)}) copy-start(f32[24,768]{1,0:T(8,128)} %mul.80) | copy-start | bytes 221188
  121.3 8.8 %copy-start.20 = (f32[24,768]{1,0:T(8,128)S(1)}, f32[24,768]{1,0:T(8,128)}, u32[]{:S(2)}) copy-start(f32[24,768]{1,0:T(8,128)} %get-tuple-element.51) | copy-start | bytes 221188
  121.3 12.2 %copy-start.7 = (f32[24,768]{1,0:T(8,128)S(1)}, f32[24,768]{1,0:T(8,128)}, u32[]{:S(2)}) copy-start(f32[24,768]{1,0:T(8,128)} %reshape.88) | copy-start | bytes 221188
  121.3 12.2 %copy-start.8 = (f32[24,768]{1,0:T(8,128)S(1)}, f32[24,768]{1,0:T(8,128)}, u32[]{:S(2)}) copy-start(f32[24,768]{1,0:T(8,128)} %mul.76) | copy-start | bytes 221188
  121.3 12.2 %copy-start.19 = (f32[24,768]{1,0:T(8,128)S(1)}, f32[24,768]{1,0:T(8,128)}, u32[]{:S(2)}) copy-start(f32[24,768]{1,0:T(8,128)} %get-tuple-element.50) | copy-start | bytes 221188
  123.2 14.8 %all-to-all-start.5 = ((f32[16,1,1152]{2,1,0:T(1,128)}), f32[16,1,1152]{2,1,0:T(1,128)S(1)}, u32[]{:S(2)}, u32[]{:S(2)}) async-start(f32[16,1,1152]{2,1,0:T(1,128)} %reshape.152), calls=%async_computation.5 | async-start | bytes 147456 | tf_op jit(solution)/shard_map/all_to_all | solution.py:105
  134.2 10.5 %copy-start.1 = (f32[251,192]{0,1:T(8,128)S(1)}, f32[251,192]{0,1:T(8,128)}, u32[]{:S(2)}) copy-start(f32[251,192]{0,1:T(8,128)} %copy.99) | copy-start | bytes 578308
  138.1 14.6 %all-to-all-start.3 = ((f32[16,1,1152]{2,1,0:T(1,128)}), f32[16,1,1152]{2,1,0:T(1,128)S(1)}, u32[]{:S(2)}, u32[]{:S(2)}) async-start(f32[16,1,1152]{2,1,0:T(1,128)} %reshape.150), calls=%async_computation.3 | async-start | bytes 147456 | tf_op jit(solution)/shard_map/all_to_all | solution.py:104
  145.7 46.9 %copy-start.22 = (f32[120]{0:T(128)S(1)}, f32[120]{0:T(128)}, u32[]{:S(2)}) copy-start(f32[120]{0:T(128)} %param.30) | copy-start | bytes 1444
  145.7 46.9 %copy-start.23 = (f32[120]{0:T(128)S(1)}, f32[120]{0:T(128)}, u32[]{:S(2)}) copy-start(f32[120]{0:T(128)} %param.25) | copy-start | bytes 1444
  145.7 85.2 %copy-start.2 = (f32[1,1,6,3072]{3,2,1,0:T(8,128)S(1)}, f32[1,1,6,3072]{3,2,1,0:T(8,128)}, u32[]{:S(2)}) copy-start(f32[1,1,6,3072]{3,2,1,0:T(8,128)} %get-tuple-element.55) | copy-start | bytes 221188
  145.7 85.9 %copy-start.5 = (f32[1,1,24,768]{3,2,1,0:T(8,128)S(1)}, f32[1,1,24,768]{3,2,1,0:T(8,128)}, u32[]{:S(2)}) copy-start(f32[1,1,24,768]{3,2,1,0:T(8,128)} %get-tuple-element.57) | copy-start | bytes 221188
  145.7 86.6 %copy-start.6 = (f32[1,1,24,768]{3,2,1,0:T(8,128)S(1)}, f32[1,1,24,768]{3,2,1,0:T(8,128)}, u32[]{:S(2)}) copy-start(f32[1,1,24,768]{3,2,1,0:T(8,128)} %get-tuple-element.59) | copy-start | bytes 221188
  152.6 80.4 %copy-start.3 = (f32[16,1,1152]{2,1,0:T(1,128)}, f32[16,1,1152]{2,1,0:T(1,128)S(1)}, u32[]{:S(2)}) copy-start(f32[16,1,1152]{2,1,0:T(1,128)S(1)} %all-to-all-done.3) | copy-start | bytes 221188
  152.6 21.8 %all-to-all-start.1 = ((f32[16,1,1152]{2,1,0:T(1,128)}), f32[16,1,1152]{2,1,0:T(1,128)S(1)}, u32[]{:S(2)}, u32[]{:S(2)}) async-start(f32[16,1,1152]{2,1,0:T(1,128)} %reshape.146), calls=%async_computation.1 | async-start | bytes 147456 | tf_op jit(solution)/shard_map/all_to_all | solution.py:103
  174.5 71.2 %all-to-all-start.6 = ((f32[251,16,48]{0,2,1:T(8,128)}), f32[251,16,48]{0,2,1:T(8,128)S(1)}, u32[]{:S(2)}, u32[]{:S(2)}) async-start(f32[251,16,48]{0,2,1:T(8,128)} %bitcast.34), calls=%async_computation.7 | async-start | bytes 1572864 | tf_op jit(solution)/shard_map/all_to_all | solution.py:123
  193.1 7.7 %collective-permute-start = (f32[120]{0:T(128)S(1)}, f32[120]{0:T(128)S(1)}, u32[]{:S(2)}, u32[]{:S(2)}) collective-permute-start(f32[120]{0:T(128)S(1)} %get-tuple-element.62), channel_id=1, source_target_pairs={{0,8},{8,16},{16,24},{24,32},{32,40},{40,48},{48,56},{56,64},{64,7... | collective-permute-start | bytes 1448 | tf_op jit(solution)/shard_map/ppermute | solution.py:16
  193.1 7.8 %collective-permute-start.8 = (f32[120]{0:T(128)S(1)}, f32[120]{0:T(128)S(1)}, u32[]{:S(2)}, u32[]{:S(2)}) collective-permute-start(f32[120]{0:T(128)S(1)} %get-tuple-element.62), channel_id=1, source_target_pairs={{0,120},{8,0},{16,8},{24,16},{32,24},{40,32},{48,40},{56,48},{64,5... | collective-permute-start | bytes 1448 | tf_op jit(solution)/shard_map/ppermute | solution.py:18
  200.9 4.2 %collective-permute-start.1 = (f32[120]{0:T(128)S(1)}, f32[120]{0:T(128)S(1)}, u32[]{:S(2)}, u32[]{:S(2)}) collective-permute-start(f32[120]{0:T(128)S(1)} %collective-permute-done), channel_id=1, source_target_pairs={{0,8},{8,16},{16,24},{24,32},{32,40},{40,48},{48,56},{56,64},{64,7... | collective-permute-start | bytes 1448 | tf_op jit(solution)/shard_map/ppermute | solution.py:16
  200.9 4.2 %collective-permute-start.9 = (f32[120]{0:T(128)S(1)}, f32[120]{0:T(128)S(1)}, u32[]{:S(2)}, u32[]{:S(2)}) collective-permute-start(f32[120]{0:T(128)S(1)} %collective-permute-done.8), channel_id=1, source_target_pairs={{0,120},{8,0},{16,8},{24,16},{32,24},{40,32},{48,40},{56,48},{64,5... | collective-permute-start | bytes 1448 | tf_op jit(solution)/shard_map/ppermute | solution.py:18
  205.0 4.2 %collective-permute-start.2 = (f32[120]{0:T(128)S(1)}, f32[120]{0:T(128)S(1)}, u32[]{:S(2)}, u32[]{:S(2)}) collective-permute-start(f32[120]{0:T(128)S(1)} %collective-permute-done.1), channel_id=1, source_target_pairs={{0,8},{8,16},{16,24},{24,32},{32,40},{40,48},{48,56},{56,64},{64,7... | collective-permute-start | bytes 1448 | tf_op jit(solution)/shard_map/ppermute | solution.py:16
  205.1 4.2 %collective-permute-start.10 = (f32[120]{0:T(128)S(1)}, f32[120]{0:T(128)S(1)}, u32[]{:S(2)}, u32[]{:S(2)}) collective-permute-start(f32[120]{0:T(128)S(1)} %collective-permute-done.9), channel_id=1, source_target_pairs={{0,120},{8,0},{16,8},{24,16},{32,24},{40,32},{48,40},{56,48},{64,5... | collective-permute-start | bytes 1448 | tf_op jit(solution)/shard_map/ppermute | solution.py:18
  209.2 4.2 %collective-permute-start.3 = (f32[120]{0:T(128)S(1)}, f32[120]{0:T(128)S(1)}, u32[]{:S(2)}, u32[]{:S(2)}) collective-permute-start(f32[120]{0:T(128)S(1)} %collective-permute-done.2), channel_id=1, source_target_pairs={{0,8},{8,16},{16,24},{24,32},{32,40},{40,48},{48,56},{56,64},{64,7... | collective-permute-start | bytes 1448 | tf_op jit(solution)/shard_map/ppermute | solution.py:16
  209.3 4.2 %collective-permute-start.11 = (f32[120]{0:T(128)S(1)}, f32[120]{0:T(128)S(1)}, u32[]{:S(2)}, u32[]{:S(2)}) collective-permute-start(f32[120]{0:T(128)S(1)} %collective-permute-done.10), channel_id=1, source_target_pairs={{0,120},{8,0},{16,8},{24,16},{32,24},{40,32},{48,40},{56,48},{64,5... | collective-permute-start | bytes 1448 | tf_op jit(solution)/shard_map/ppermute | solution.py:18
  213.4 4.2 %collective-permute-start.4 = (f32[120]{0:T(128)S(1)}, f32[120]{0:T(128)S(1)}, u32[]{:S(2)}, u32[]{:S(2)}) collective-permute-start(f32[120]{0:T(128)S(1)} %collective-permute-done.3), channel_id=1, source_target_pairs={{0,8},{8,16},{16,24},{24,32},{32,40},{40,48},{48,56},{56,64},{64,7... | collective-permute-start | bytes 1448 | tf_op jit(solution)/shard_map/ppermute | solution.py:16
  213.5 4.2 %collective-permute-start.12 = (f32[120]{0:T(128)S(1)}, f32[120]{0:T(128)S(1)}, u32[]{:S(2)}, u32[]{:S(2)}) collective-permute-start(f32[120]{0:T(128)S(1)} %collective-permute-done.11), channel_id=1, source_target_pairs={{0,120},{8,0},{16,8},{24,16},{32,24},{40,32},{48,40},{56,48},{64,5... | collective-permute-start | bytes 1448 | tf_op jit(solution)/shard_map/ppermute | solution.py:18
  217.6 4.2 %collective-permute-start.5 = (f32[120]{0:T(128)S(1)}, f32[120]{0:T(128)S(1)}, u32[]{:S(2)}, u32[]{:S(2)}) collective-permute-start(f32[120]{0:T(128)S(1)} %collective-permute-done.4), channel_id=1, source_target_pairs={{0,8},{8,16},{16,24},{24,32},{32,40},{40,48},{48,56},{56,64},{64,7... | collective-permute-start | bytes 1448 | tf_op jit(solution)/shard_map/ppermute | solution.py:16
  217.6 4.2 %collective-permute-start.13 = (f32[120]{0:T(128)S(1)}, f32[120]{0:T(128)S(1)}, u32[]{:S(2)}, u32[]{:S(2)}) collective-permute-start(f32[120]{0:T(128)S(1)} %collective-permute-done.12), channel_id=1, source_target_pairs={{0,120},{8,0},{16,8},{24,16},{32,24},{40,32},{48,40},{56,48},{64,5... | collective-permute-start | bytes 1448 | tf_op jit(solution)/shard_map/ppermute | solution.py:18
  221.7 4.2 %collective-permute-start.6 = (f32[120]{0:T(128)S(1)}, f32[120]{0:T(128)S(1)}, u32[]{:S(2)}, u32[]{:S(2)}) collective-permute-start(f32[120]{0:T(128)S(1)} %collective-permute-done.5), channel_id=1, source_target_pairs={{0,8},{8,16},{16,24},{24,32},{32,40},{40,48},{48,56},{56,64},{64,7... | collective-permute-start | bytes 1448 | tf_op jit(solution)/shard_map/ppermute | solution.py:16
  221.8 4.2 %collective-permute-start.14 = (f32[120]{0:T(128)S(1)}, f32[120]{0:T(128)S(1)}, u32[]{:S(2)}, u32[]{:S(2)}) collective-permute-start(f32[120]{0:T(128)S(1)} %collective-permute-done.13), channel_id=1, source_target_pairs={{0,120},{8,0},{16,8},{24,16},{32,24},{40,32},{48,40},{56,48},{64,5... | collective-permute-start | bytes 1448 | tf_op jit(solution)/shard_map/ppermute | solution.py:18
  225.9 4.2 %collective-permute-start.7 = (f32[120]{0:T(128)S(1)}, f32[120]{0:T(128)S(1)}, u32[]{:S(2)}, u32[]{:S(2)}) collective-permute-start(f32[120]{0:T(128)S(1)} %collective-permute-done.6), channel_id=1, source_target_pairs={{0,8},{8,16},{16,24},{24,32},{32,40},{40,48},{48,56},{56,64},{64,7... | collective-permute-start | bytes 1448 | tf_op jit(solution)/shard_map/ppermute | solution.py:16
  236.2 1.5 copy-start.4
Sparse Core Ops, SparseCore 0:
  48.4 56.0 all-reduce.2
  108.1 30.1 reduce-scatter.1
